TPU v7x, 128 devices: a whole 4x4x4 slice. The times are simulated.
128 devices in a mesh: aa: 16 (over y, x), ba: 8 (over z, core).
Axes of the slice: x: 4, y: 4, z: 4, core: 2. Of those that a mesh axis runs over, the one named last changes fastest.
Arguments:
- queries: bfloat16 [8, 128, 8192], P('ba', None, 'aa'), may hold values from -10 to 10
- new_kv: bfloat16 [8, 128, 2, 512], P('ba', 'aa'), may hold values from -4 to 4
- pool: bfloat16 [8, 192, 32, 2, 512], P('ba', 'aa'), may hold values from -4 to 4
- page_table: int32 [8, 64], P('ba', 'aa'), may hold values from 0 to 11, as said below
- ctx_len: int32 [8, 16], P('ba', 'aa'), may hold values from 1 to 128, as said below
- move_page: int32 [8, 112], P('ba', 'aa'), may hold values from 0 to 11, as said below
- move_dest: int32 [8, 112], P('ba', 'aa'), may hold values from 0 to 7, as said below
- append_page: int32 [8, 16], P('ba', 'aa'), may hold values from 0 to 11
Outputs:
- attended: bfloat16 [8, 128, 8192], P('ba', None, 'aa')
- pool_out: bfloat16 [8, 192, 32, 2, 512], P('ba', 'aa')
Inputs may be any that keep to these rules, and one draw needn't show every extreme that they name: `page_table`: the entries of one device are distinct pages of its pool and differ from its leaving pages and its append page. `ctx_len`: for each instance some index of aa holds exactly 128 live rows. `move_page`: the 7 entries of one device are distinct pages of its pool. `move_dest`: A device never names its own instance and names any one instance at most 2 times; for each index of aa one instance is named exactly 2 times by the device of every other instance.
All inputs are finite; a program needn't handle non-finite values.
Results may differ from a plain program's by a relative error of at most 0.0017.
Values may be sent and summed in bfloat16 or wider, within the bound.
No kernel may reach another device: no remote copies, remote signals or barrier semaphores. Data moves between devices by JAX's collectives and lax.ppermute only.
A program may use at most 64 MiB of HBM per device.

v0:
```python
import math
import jax
import jax.numpy as jnp
from jax import lax
from jax.sharding import PartitionSpec as P

HEAD_DIM = 128
MOST = 2
NEG_LARGE = -1e30


def in_one_piece(arrays, axis, split_dim, concat_dim, along):
    widths = [math.prod(a.shape[along:]) for a in arrays]
    both = jnp.concatenate(
        [a.reshape(*a.shape[:along], w) for a, w in zip(arrays, widths)], axis=along
    )
    filled = lax.all_to_all(both, axis, split_axis=split_dim, concat_axis=concat_dim, tiled=True)
    blocks = jnp.split(filled, [sum(widths[:k]) for k in range(1, len(widths))], axis=along)
    return tuple(
        (b.reshape(*filled.shape[:along], *a.shape[along:]) for a, b in zip(arrays, blocks))
    )


def from_everyone(value, axis):
    length = lax.axis_size(axis)
    return lax.all_to_all(
        jnp.broadcast_to(value[None], (length, *value.shape)), axis, 0, 0, tiled=True
    )


def taken_together(value, axis):
    return from_everyone(value, axis).max(axis=0)


def split_up(value, dim, length):
    lengths = value.shape
    blocks = value.reshape(*lengths[:dim], length, lengths[dim] // length, *lengths[dim + 1 :])
    return jnp.moveaxis(blocks, dim, 0)


def sum_at_owner(value, axis, dim):
    length = lax.axis_size(axis)
    blocks = lax.all_to_all(split_up(value, dim, length), axis, 0, 0, tiled=True)
    return jnp.sum(blocks, axis=0)


def in_one_piece_2(arrays, axis, dim, along):
    widths = [math.prod(a.shape[along:]) for a in arrays]
    both = jnp.concatenate(
        [a.reshape(*a.shape[:along], w) for a, w in zip(arrays, widths)], axis=along
    )
    filled = sum_at_owner(both, axis, dim)
    blocks = jnp.split(filled, [sum(widths[:k]) for k in range(1, len(widths))], axis=along)
    return tuple(
        (b.reshape(*filled.shape[:along], *a.shape[along:]) for a, b in zip(arrays, blocks))
    )


def block_plan(total_rows):
    counted = max(1, total_rows // 512)
    length = -(-total_rows // counted)
    length = -(-length // 8) * 8
    return (counted, length)


def combine_parts(former, latter):
    former_max, former_sum, former_out = former
    latter_max, latter_sum, latter_out = latter
    joint_max = jnp.maximum(former_max, latter_max)
    former_scale = jnp.exp(former_max - joint_max)
    latter_scale = jnp.exp(latter_max - joint_max)
    joint_sum = former_sum * former_scale + latter_sum * latter_scale
    joint_out = former_out * former_scale[..., None] + latter_out * latter_scale[..., None]
    return (joint_max, joint_sum, joint_out)


def attend_rows(query_heads, key_rows, visible):
    total_rows = key_rows.shape[0]
    counted, length = block_plan(total_rows)
    query_count, kv_heads, group_size, head_dim = query_heads.shape
    blocked_keys = key_rows.reshape(counted, length, 2, kv_heads, head_dim)
    blocked_mask = visible.reshape(query_count, counted, length).transpose(1, 0, 2)
    scale = 1.0 / math.sqrt(head_dim)

    def block_step(state_now, inputs):
        run_max, run_sum, run_out = state_now
        block_keys, block_mask = inputs
        scores = (
            jnp.einsum(
                "qkgd,rkd->qkgr", query_heads, block_keys[:, 0], preferred_element_type=jnp.float32
            )
            * scale
        )
        allowed = block_mask[:, None, None, :]
        scores = jnp.where(allowed, scores, NEG_LARGE)
        new_max = jnp.maximum(run_max, jnp.max(scores, axis=-1))
        weights = jnp.where(allowed, jnp.exp(scores - new_max[..., None]), 0.0)
        shrink = jnp.exp(run_max - new_max)
        new_sum = run_sum * shrink + jnp.sum(weights, axis=-1)
        block_values = block_keys[:, 1].astype(jnp.float32)
        new_out = run_out * shrink[..., None] + jnp.einsum(
            "qkgr,rkd->qkgd", weights, block_values, precision=lax.Precision.HIGHEST
        )
        return ((new_max, new_sum, new_out), None)

    start_state = (
        jnp.full((query_count, kv_heads, group_size), NEG_LARGE, jnp.float32),
        jnp.zeros((query_count, kv_heads, group_size), jnp.float32),
        jnp.zeros((query_count, kv_heads, group_size, head_dim), jnp.float32),
    )
    finished, _ = lax.scan(block_step, start_state, (blocked_keys, blocked_mask))
    return finished


def local(queries, new_kv, pool, page_table, ctx_len, move_page, move_dest, append_page):
    instances = lax.axis_size("ba")
    position = lax.axis_index("aa")
    pool_pages = pool[0]
    page_rows = pool_pages.shape[1]
    kv_width = pool_pages.shape[-1]
    kv_heads = kv_width // HEAD_DIM
    gathered = lax.all_gather(queries[0], "aa", axis=1, tiled=True)
    query_count = gathered.shape[0]
    query_heads = gathered.reshape(query_count, kv_heads, -1, HEAD_DIM)
    moved_ids = move_page[0]
    targets = move_dest[0]
    move_count = moved_ids.shape[0]
    counter = jnp.arange(move_count, dtype=jnp.int32)
    earlier = (counter[None, :] < counter[:, None]) & (targets[None, :] == targets[:, None])
    slot_index = targets * MOST + jnp.sum(earlier, axis=1)
    select = (jnp.arange(instances * MOST, dtype=jnp.int32)[:, None] == slot_index[None, :]).astype(
        jnp.bfloat16
    )
    picked = jnp.take(pool_pages, moved_ids, axis=0).reshape(move_count, -1)
    outgoing = jnp.dot(select, picked, preferred_element_type=jnp.float32).astype(jnp.bfloat16)
    outgoing = outgoing.reshape(instances, MOST, page_rows, 2, kv_width)
    occupied = (
        jnp.sum(select.astype(jnp.float32), axis=1).astype(jnp.bfloat16).reshape(instances, MOST)
    )
    incoming, arrived = in_one_piece((outgoing, occupied), "ba", 0, 0, 2)
    moved_rows = incoming.reshape(-1, 2, kv_width)
    moved_live = jnp.broadcast_to(
        (arrived > 0.5)[:, :, None], (instances, MOST, page_rows)
    ).reshape(-1)
    resident = jnp.take(pool_pages, page_table[0], axis=0).reshape(-1, 2, kv_width)
    resident_live = jnp.arange(resident.shape[0], dtype=jnp.int32) < ctx_len[0, 0]
    fresh_rows = new_kv[0]
    fresh_count = fresh_rows.shape[0]
    fresh_place = position * fresh_count + jnp.arange(fresh_count, dtype=jnp.int32)
    fresh_visible = fresh_place[None, :] <= jnp.arange(query_count, dtype=jnp.int32)[:, None]
    resident_visible = jnp.broadcast_to(
        resident_live[None, :], (query_count, resident_live.shape[0])
    )
    moved_visible = jnp.broadcast_to(moved_live[None, :], (query_count, moved_live.shape[0]))
    local_part = attend_rows(
        query_heads,
        jnp.concatenate([resident, fresh_rows], axis=0),
        jnp.concatenate([resident_visible, fresh_visible], axis=1),
    )
    moved_part = attend_rows(query_heads, moved_rows, moved_visible)
    partials = combine_parts(local_part, moved_part)
    run_max, run_sum, run_out = partials
    top_max = taken_together(run_max, "aa")
    rescale = jnp.exp(run_max - top_max)
    numerator = (run_out * rescale[..., None]).reshape(query_count, -1, HEAD_DIM)
    denominator = (run_sum * rescale).reshape(query_count, -1)
    numerator, denominator = in_one_piece_2((numerator, denominator), "aa", 1, 2)
    result = numerator / denominator[..., None]
    attended = result.reshape(1, query_count, -1).astype(jnp.bfloat16)
    zero = jnp.zeros((), jnp.int32)
    updated = lax.dynamic_update_slice(
        pool_pages, fresh_rows[None], (append_page[0, 0], zero, zero, zero)
    )
    return (attended, updated[None])


def solution(mesh):
    return jax.shard_map(
        local,
        mesh=mesh,
        in_specs=(
            P("ba", None, "aa"),
            P("ba", "aa", None, None),
            P("ba", "aa", None, None, None),
            P("ba", "aa"),
            P("ba", "aa"),
            P("ba", "aa"),
            P("ba", "aa"),
            P("ba", "aa"),
        ),
        out_specs=(P("ba", None, "aa"), P("ba", "aa", None, None, None)),
        check_vma=False,
    )
```

profile of v0, /device:TPU:0, one launch (start us, length us, event | category | flops | bytes accessed | tf_op | source)
XLA Modules:
  0.0 190.3 jit_solution(174172654630481055)
XLA Ops:
  7.2 0.0 all-gather.3.cloned.1.call-start
  7.2 1.1 copy.173
  8.3 1.7 copy.132
  10.0 0.0 all-gather.3.cloned.1.call-update
  10.0 0.7 fusion.45
  10.7 0.7 compare_and_fusion
  11.4 0.9 convert_reduce_fusion
  12.3 0.7 fusion.46
  12.9 0.1 fusion.42
  13.0 0.1 reshape_reshape.9
  13.1 1.5 gather_fusion.1
  14.6 0.3 gather.15
  14.9 0.6 convolution_convert_fusion
  15.5 0.7 reshape_reshape.7
  16.2 1.9 %pad_maximum_fusion = bf16[8,2,32769]{2,1,0:T(2,128)(2,1)} fusion(bf16[8,2,1]{2,1,0:T(2,128)(2,1)S(1)} %reshape_reshape.9, bf16[8,2,32768]{2,1,0:T(2,128)(2,1)S(1)} %reshape_reshape.7), kind=kLoop, calls=%fused_computation.33 | loop fusion | flops 2097216 | bytes 2097216 | tf_op jit(solution)/shard_map/concatenate | solution.py:14
  18.2 5.4 %all-to-all-start = ((bf16[8,2,32769]{2,1,0:T(2,128)(2,1)}), bf16[8,2,32769]{2,1,0:T(2,128)(2,1)S(1)}, u32[]{:S(2)}, u32[]{:S(2)}) async-start(bf16[8,2,32769]{2,1,0:T(2,128)(2,1)} %pad_maximum_fusion), calls=%async_computation | async-start | bytes 2105344 | tf_op jit(solution)/shard_map/all_to_all | solution.py:17
  24.3 0.1 broadcast_in_dim.123
  24.4 0.1 broadcast_in_dim.124
  24.5 1.1 gather_fusion
  25.6 0.2 reshape.297
  25.8 0.1 iota_compare_fusion.3
  25.8 0.1 pad_add_fusion
  25.9 0.1 copy_select_fusion
  26.0 13.6 %all-to-all-done = bf16[8,2,32769]{2,1,0:T(2,128)(2,1)S(1)} async-done(((bf16[8,2,32769]{2,1,0:T(2,128)(2,1)}), bf16[8,2,32769]{2,1,0:T(2,128)(2,1)S(1)}, u32[]{:S(2)}, u32[]{:S(2)}) %all-to-all-start) | async-done | bytes 1048640 | tf_op jit(solution)/shard_map/all_to_all | solution.py:17
  39.6 0.1 copy.156
  39.7 0.7 split.17
  40.4 0.8 squeeze.63
  41.3 0.4 fusion.58
  41.6 1.1 copy.158
  42.8 0.1 copy.136
  42.9 0.1 broadcast_in_dim.132
  42.9 0.1 broadcast_in_dim.133
  43.0 15.0 %all-gather.3.cloned.1.call-done = bf16[1,128,8192]{1,2,0:T(8,128)(2,1)} async-done(((bf16[1,128,512]{1,2,0:T(8,128)(2,1)}), bf16[1,128,8192]{1,2,0:T(8,128)(2,1)}) %all-gather.3.cloned.1.call-update) | async-done | bytes 2097168 | tf_op jit(solution)/shard_map/all_gather | solution.py:122
  58.1 8.9 %bitcast_reduce_fusion = (f32[128,4,16]{0,2,1:T(8,128)S(1)}, f32[4,512,128,16]{2,1,3,0:T(8,128)}) fusion(pred[512]{0:T(512)(128)(4,1)S(1)} %broadcast_in_dim.133, bf16[128,4,16,128]{0,3,2,1:T(8,128)(2,1)} %bitcast.111, bf16[512,1,4,128]{3,2,1,0:T(4,128)(2,1)S(1)} %get-tuple-element.59), kind=kOutput, calls=%fused_computation.4 | convolution fusion | flops 1086316544 | bytes 19431936 | tf_op jit(solution)/shard_map/while/body/eval_jaxpr/qkgd,rkd->qkgr/dot_general | solution.py:89
  66.9 2.9 %fusion.15 = (f32[128,4,16]{0,2,1:T(8,128)S(1)}, f32[4,136,128,16]{2,1,3,0:T(8,128)}) fusion(pred[128,136]{0,1:T(8,128)(4,1)S(1)} %pad_add_fusion, bf16[128,4,16,128]{0,3,2,1:T(8,128)(2,1)S(1)} %bitcast.112, bf16[128,2,4,128]{3,0,2,1:T(8,128)(2,1)S(1)} %copy_select_fusion, bf16[8,2,4,128]{3,0,2,1:T(8,128)(2,1)S(1)} %copy.131), kind=kOutput, calls=%fused_computation.25 | convolution fusion | flops 288825344 | bytes 6882304 | tf_op jit(solution)/shard_map/while/body/eval_jaxpr/qkgd,rkd->qkgr/dot_general | solution.py:89
  69.8 0.8 broadcast_in_dim.138
  70.7 5.1 %all-to-all-start.1 = ((f32[16,128,4,16]{1,3,2,0:T(8,128)}), f32[16,128,4,16]{1,3,2,0:T(8,128)S(1)}, u32[]{:S(2)}, u32[]{:S(2)}) async-start(f32[16,128,4,16]{1,3,2,0:T(8,128)} %broadcast_in_dim.138), calls=%async_computation.1 | async-start | bytes 1048576 | tf_op jit(solution)/shard_map/all_to_all | solution.py:26
  75.8 8.5 %fusion.2 = f32[128,4,16]{0,2,1:T(8,128)S(1)} fusion(f32[4,512,128,16]{2,1,3,0:T(8,128)} %get-tuple-element.69, f32[128,4,16]{0,2,1:T(8,128)S(1)} %get-tuple-element.62, pred[512]{0:T(512)(128)(4,1)S(1)} %broadcast_in_dim.133), kind=kLoop, calls=%fused_computation.8 | loop fusion | flops 20963328 | bytes 16843264 | tf_op jit(solution)/shard_map/while/body/eval_jaxpr/reduce_sum | solution.py:99
  84.3 1.3 fusion.16
  85.7 5.3 %fusion.17 = f32[4,128,128,16]{2,1,3,0:T(8,128)} fusion(f32[4,136,128,16]{2,1,3,0:T(8,128)S(1)} %bitcast.110, f32[128,4,16]{0,2,1:T(8,128)S(1)} %get-tuple-element.65, pred[128,136]{0,1:T(8,128)(4,1)S(1)} %pad_add_fusion, bf16[8,2,4,128]{3,0,2,1:T(8,128)(2,1)S(1)} %copy.131, bf16[128,2,4,128]{3,0,2,1:T(8,128)(2,1)S(1)} %copy_select_fusion), kind=kOutput, calls=%fused_computation.27 | convolution fusion | flops 1716011008 | bytes 8979456 | tf_op jit(solution)/shard_map/while/body/eval_jaxpr/qkgr,rkd->qkgd/dot_general | solution.py:101
  91.0 15.8 %fusion.13 = f32[128,4,16,128]{0,3,2,1:T(8,128)S(1)} fusion(f32[4,128,128,16]{2,1,3,0:T(8,128)} %fusion.17, f32[4,512,128,16]{2,1,3,0:T(8,128)} %get-tuple-element.69, f32[128,4,16]{0,2,1:T(8,128)S(1)} %get-tuple-element.62, pred[512]{0:T(512)(128)(4,1)S(1)} %broadcast_in_dim.133, f32[128,4,16]{0,2,1:T(8,128)S(1)} %get-tuple-element.64, ...), kind=kOutput, calls=%fused_computation.22 | convolution fusion | flops 6465519616 | bytes 25887232 | tf_op jit(solution)/shard_map/while/body/eval_jaxpr/qkgr,rkd->qkgd/dot_general | solution.py:101
  106.8 2.8 %copy.141 = f32[128,16,4,128]{0,2,3,1:T(4,128)S(1)} copy(f32[128,16,4,128]{0,3,2,1:T(8,128)S(1)} %bitcast.113) | data formatting | bytes 8388608 | tf_op jit(solution)/shard_map/concatenate | solution.py:49
  109.6 0.1 exponential_multiply_fusion
  109.6 3.0 %maximum_bitcast_fusion = f32[16,128,4,129]{1,2,3,0:T(4,128)} fusion(f32[128,16,4,1]{0,2,3,1:T(4,128)S(1)} %exponential_multiply_fusion, f32[128,16,4,128]{0,2,3,1:T(4,128)S(1)} %copy.141), kind=kLoop, calls=%fused_computation.18 | loop fusion | flops 1056768 | bytes 8454144 | tf_op jit(solution)/shard_map/transpose | solution.py:38
  112.6 7.3 %all-to-all-start.2 = ((f32[16,128,4,129]{1,2,3,0:T(4,128)}), f32[16,128,4,129]{1,2,3,0:T(4,128)}, u32[]{:S(2)}, u32[]{:S(2)}) async-start(f32[16,128,4,129]{1,2,3,0:T(4,128)} %maximum_bitcast_fusion), calls=%async_computation.2 | async-start | bytes 8454144 | tf_op jit(solution)/shard_map/all_to_all | solution.py:43
  120.5 59.2 %all-to-all-done.2 = f32[16,128,4,129]{1,2,3,0:T(4,128)} async-done(((f32[16,128,4,129]{1,2,3,0:T(4,128)}), f32[16,128,4,129]{1,2,3,0:T(4,128)}, u32[]{:S(2)}, u32[]{:S(2)}) %all-to-all-start.2) | async-done | bytes 4227104 | tf_op jit(solution)/shard_map/all_to_all | solution.py:43
  179.7 2.9 %reduce_sum.63 = f32[128,4,129]{0,1,2:T(4,128)S(1)} reduce(f32[16,128,4,129]{1,2,3,0:T(4,128)} %all-to-all-done.2, f32[]{:T(128)} %constant.52.clone.1), dimensions={0}, to_apply=%region_7.8 | reduce | flops 990720 | bytes 4491268 | tf_op jit(solution)/shard_map/reduce_sum | solution.py:44
  182.6 0.8 copy.143
  (34 shorter events, 0.3 us)
Async XLA Ops:
  7.2 50.9 %all-gather.3.cloned.1.call-start = ((), (), s32[]{:S(2)}) async-start(), calls=%async_computation.3 | async-start | bytes 2228224 | tf_op jit(solution)/shard_map/all_gather | solution.py:122
  14.6 9.0 %copy-start.4 = (s32[1,4]{1,0:T(1,128)S(1)}, s32[1,4]{1,0:T(1,128)}, u32[]{:S(2)}) copy-start(s32[1,4]{1,0:T(1,128)} %param.11) | copy-start | bytes 52
  14.6 9.8 %copy-start.3 = (bf16[1,8,2,512]{3,2,1,0:T(2,128)(2,1)S(1)}, bf16[1,8,2,512]{3,2,1,0:T(2,128)(2,1)}, u32[]{:S(2)}) copy-start(bf16[1,8,2,512]{3,2,1,0:T(2,128)(2,1)} %param.9) | copy-start | bytes 49156
  18.2 21.4 %all-to-all-start = ((bf16[8,2,32769]{2,1,0:T(2,128)(2,1)}), bf16[8,2,32769]{2,1,0:T(2,128)(2,1)S(1)}, u32[]{:S(2)}, u32[]{:S(2)}) async-start(bf16[8,2,32769]{2,1,0:T(2,128)(2,1)} %pad_maximum_fusion), calls=%async_computation | async-start | bytes 2105344 | tf_op jit(solution)/shard_map/all_to_all | solution.py:17
  58.0 8.9 %copy-start = (bf16[1,128,8192]{1,2,0:T(8,128)(2,1)S(1)}, bf16[1,128,8192]{1,2,0:T(8,128)(2,1)}, u32[]{:S(2)}) copy-start(bf16[1,128,8192]{1,2,0:T(8,128)(2,1)} %all-gather.3.cloned.1.call-done) | copy-start | bytes 6291460
  70.7 13.6 %slice-start = ((s8[4456448]{0:T(1024)(128)(4,1)}), s8[262144]{0:T(1024)(128)(4,1)S(1)}, s32[]{:S(2)}) async-start(s8[4456448]{0:T(1024)(128)(4,1)} %bitcast.109), calls=%async_computation.4 | async-start | bytes 524288
  70.7 20.2 %all-to-all-start.1 = ((f32[16,128,4,16]{1,3,2,0:T(8,128)}), f32[16,128,4,16]{1,3,2,0:T(8,128)S(1)}, u32[]{:S(2)}, u32[]{:S(2)}) async-start(f32[16,128,4,16]{1,3,2,0:T(8,128)} %broadcast_in_dim.138), calls=%async_computation.1 | async-start | bytes 1048576 | tf_op jit(solution)/shard_map/all_to_all | solution.py:26
  75.8 8.6 %slice-start.1 = ((s8[4456448]{0:T(1024)(128)(4,1)}), s8[4194304]{0:T(1024)(128)(4,1)S(1)}, s32[]{:S(2)}) async-start(s8[4456448]{0:T(1024)(128)(4,1)} %bitcast.109), calls=%async_computation.5 | async-start | bytes 8388608
  85.6 5.3 %copy-start.2 = (bf16[512,1,4,128]{0,3,2,1:T(8,128)(2,1)S(1)}, bf16[512,1,4,128]{0,3,2,1:T(8,128)(2,1)}, u32[]{:S(2)}) copy-start(bf16[512,1,4,128]{0,3,2,1:T(8,128)(2,1)} %copy.158) | copy-start | bytes 1572868
  112.6 67.1 %all-to-all-start.2 = ((f32[16,128,4,129]{1,2,3,0:T(4,128)}), f32[16,128,4,129]{1,2,3,0:T(4,128)}, u32[]{:S(2)}, u32[]{:S(2)}) async-start(f32[16,128,4,129]{1,2,3,0:T(4,128)} %maximum_bitcast_fusion), calls=%async_computation.2 | async-start | bytes 8454144 | tf_op jit(solution)/shard_map/all_to_all | solution.py:43
  120.5 62.9 %copy-start.1 = (bf16[1,12,32,2,512]{4,3,2,1,0:T(2,128)(2,1)}, bf16[1,12,32,2,512]{4,3,2,1,0:T(2,128)(2,1)S(1)}, u32[]{:S(2)}) copy-start(bf16[1,12,32,2,512]{4,3,2,1,0:T(2,128)(2,1)S(1)} %bitcast_dynamic-update-slice_fusion) | copy-start | bytes 2359300
Sparse Core Ops, SparseCore 0:
  10.7 47.2 all-gather.2
where the time goes:
time: 191 us; the launch traced here: 190 us
  waiting for transfers between devices  87.8 us (46%)
  matrix products  33.4 us (17%)
  other arithmetic  21 us (11%)
  starting transfers between devices  17.8 us (9%)
  between operations  15.6 us (8%)
  local copies, waits for them, and re-layouts  14.7 us (8%)
    all_to_all x1, waiting for transfers between devices, sum_at_owner(): lax.all_to_all(split_up(value, dim, length), axis, 0, 0, tiled=True)  59.2 us
    dot_general x2, matrix products, block_step(): jnp.einsum('qkgr,rkd->qkgd', weights, block_values, precision=lax.Precisi...  21 us
    all_gather x1, waiting for transfers between devices, local(): gathered = lax.all_gather(queries[0], 'aa', axis=1, tiled=True)  15 us
    all_to_all x1, waiting for transfers between devices, in_one_piece(): lax.all_to_all(both, axis, split_axis=split_dim, concat_axis=concat_dim,...  13.6 us
    dot_general x2, matrix products, block_step(): jnp.einsum('qkgd,rkd->qkgr', query_heads, block_keys[:, 0], preferred_ele...  11.8 us
    reduce_sum x2, other arithmetic, block_step(): new_sum = run_sum * shrink + jnp.sum(weights, axis=-1)  9.83 us
    all_to_all x1, starting transfers between devices, sum_at_owner(): lax.all_to_all(split_up(value, dim, length), axis, 0, 0, tiled=True)  7.25 us
    all_to_all x1, starting transfers between devices, in_one_piece(): lax.all_to_all(both, axis, split_axis=split_dim, concat_axis=concat_dim,...  5.39 us
  transfers between devices with their start and end apart: 4, of which 3 were waited for; matrix products, arithmetic and copies ran while one was open for 15% of the time, Pallas kernels for 0%

commit v1 on v0

--- a/solution.py
+++ b/solution.py
@@ -119,7 +119,11 @@
     page_rows = pool_pages.shape[1]
     kv_width = pool_pages.shape[-1]
     kv_heads = kv_width // HEAD_DIM
-    gathered = lax.all_gather(queries[0], "aa", axis=1, tiled=True)
+    extend_the_types = lambda payload: jnp.concatenate(
+        lax.all_to_all(jnp.stack([payload for _ in range(lax.psum(1, "aa"))], axis=0), "aa", 0, 0),
+        1,
+    )
+    gathered = extend_the_types(queries[0])
     query_count = gathered.shape[0]
     query_heads = gathered.reshape(query_count, kv_heads, -1, HEAD_DIM)
     moved_ids = move_page[0]

time: 191 us -> 197 us (1.031)
  between operations: 15.6 us -> 2.23 us
  waiting for transfers between devices: 87.8 us -> 95 us
  local copies, waits for them, and re-layouts: 14.7 us -> 20.6 us
  starting transfers between devices: 17.8 us -> 23.5 us
    all_to_all x0 -> x1, waiting for transfers between devices: none -> 19.2 us  [local(): lax.all_to_all(jnp.stack([payload for _ in range(lax.psum(1, 'aa'))], axi...]
    all_gather x1 -> x0, waiting for transfers between devices: 15 us -> none  [local(): gathered = lax.all_gather(queries[0], 'aa', axis=1, tiled=True)]
    all_to_all x0 -> x1, starting transfers between devices: none -> 7.03 us  [local(): lax.all_to_all(jnp.stack([payload for _ in range(lax.psum(1, 'aa'))], axi...]
    all_to_all x1, waiting for transfers between devices: 13.6 us -> 15.9 us  [in_one_piece(): lax.all_to_all(both, axis, split_axis=split_dim, concat_axis=concat_dim,...]
    unnamed x19 -> x16, local copies, waits for them, and re-layouts: 4.82 us -> 3.34 us
  transfers between devices with their start and end apart: 4 -> 4, of which waited for: 3 -> 3; matrix products, arithmetic and copies ran while one was open for 15% -> 14% of each run, Pallas kernels for 0% -> 0%
where the time goes in v1:
time: 197 us; the launch traced here: 196 us
  waiting for transfers between devices  95 us (48%)
  matrix products  32.6 us (17%)
  starting transfers between devices  23.5 us (12%)
  other arithmetic  22 us (11%)
  local copies, waits for them, and re-layouts  20.6 us (10%)
  between operations  2.23 us (1%)
    all_to_all x1, waiting for transfers between devices, sum_at_owner(): lax.all_to_all(split_up(value, dim, length), axis, 0, 0, tiled=True)  59.9 us
    dot_general x2, matrix products, block_step(): jnp.einsum('qkgr,rkd->qkgd', weights, block_values, precision=lax.Precisi...  21 us
    all_to_all x1, waiting for transfers between devices, local(): lax.all_to_all(jnp.stack([payload for _ in range(lax.psum(1, 'aa'))], axi...  19.2 us
    all_to_all x1, waiting for transfers between devices, in_one_piece(): lax.all_to_all(both, axis, split_axis=split_dim, concat_axis=concat_dim,...  15.9 us
    dot_general x2, matrix products, block_step(): jnp.einsum('qkgd,rkd->qkgr', query_heads, block_keys[:, 0], preferred_ele...  11 us
    reduce_sum x2, other arithmetic, block_step(): new_sum = run_sum * shrink + jnp.sum(weights, axis=-1)  9.83 us
    all_to_all x1, starting transfers between devices, local(): lax.all_to_all(jnp.stack([payload for _ in range(lax.psum(1, 'aa'))], axi...  7.03 us
    all_to_all x1, starting transfers between devices, sum_at_owner(): lax.all_to_all(split_up(value, dim, length), axis, 0, 0, tiled=True)  7.01 us
  transfers between devices with their start and end apart: 4, of which 3 were waited for; matrix products, arithmetic and copies ran while one was open for 14% of the time, Pallas kernels for 0%

profile of v1, /device:TPU:0, one launch (start us, length us, event | category | flops | bytes accessed | tf_op | source)
XLA Modules:
  0.0 195.8 jit_solution(16042661867917780158)
XLA Ops:
  0.6 1.1 copy.173
  1.8 0.7 fusion.45
  2.4 0.7 compare_and_fusion
  3.1 0.9 convert_reduce_fusion
  4.0 0.7 fusion.46
  4.7 0.1 fusion.42
  4.8 0.1 reshape_reshape.13
  4.8 1.5 gather_fusion.1
  6.4 0.3 gather.15
  6.7 0.6 convolution_convert_fusion
  7.3 0.7 reshape_reshape.11
  8.0 1.9 pad_maximum_fusion
  9.9 5.5 %all-to-all-start.1 = ((bf16[8,2,32769]{2,1,0:T(2,128)(2,1)}), bf16[8,2,32769]{2,1,0:T(2,128)(2,1)S(1)}, u32[]{:S(2)}, u32[]{:S(2)}) async-start(bf16[8,2,32769]{2,1,0:T(2,128)(2,1)} %pad_maximum_fusion), calls=%async_computation.1 | async-start | bytes 2105344 | tf_op jit(solution)/shard_map/all_to_all | solution.py:17
  15.5 0.1 copy.132
  15.6 15.9 %all-to-all-done.1 = bf16[8,2,32769]{2,1,0:T(2,128)(2,1)S(1)} async-done(((bf16[8,2,32769]{2,1,0:T(2,128)(2,1)}), bf16[8,2,32769]{2,1,0:T(2,128)(2,1)S(1)}, u32[]{:S(2)}, u32[]{:S(2)}) %all-to-all-start.1) | async-done | bytes 1048640 | tf_op jit(solution)/shard_map/all_to_all | solution.py:17
  31.5 1.8 stack.3
  33.2 7.0 %all-to-all-start = ((bf16[16,128,512]{1,2,0:T(8,128)(2,1)}), bf16[16,128,512]{1,2,0:T(8,128)(2,1)S(1)}, u32[]{:S(2)}, u32[]{:S(2)}) async-start(bf16[16,128,512]{1,2,0:T(8,128)(2,1)} %stack.3), calls=%async_computation | async-start | bytes 4194304 | tf_op jit(solution)/shard_map/all_to_all | solution.py:123
  40.9 0.1 broadcast_in_dim.123
  41.0 0.1 broadcast_in_dim.124
  41.2 2.2 %gather_fusion = bf16[4,32,2,512]{3,2,1,0:T(2,128)(2,1)S(1)} fusion(bf16[12,32,2,512]{3,2,1,0:T(2,128)(2,1)} %bitcast.118, s32[1024]{0:T(1024)S(1)} %pad_clamp_fusion.1), kind=kCustom, calls=%fused_computation | custom fusion | bytes 524304 | tf_op jit(solution)/shard_map/jit(_take)/gather | solution.py:149
  43.4 0.9 reshape.296
  44.3 0.1 iota_compare_fusion.3
  44.4 0.1 pad_add_fusion
  44.5 1.0 copy_select_fusion
  45.5 0.1 copy.156
  45.6 1.8 split.17
  47.4 1.8 squeeze.59
  49.3 1.3 fusion.58
  50.6 1.3 copy.158
  51.9 0.1 copy.136
  52.0 0.1 broadcast_in_dim.132
  52.1 0.1 broadcast_in_dim.133
  52.2 19.2 %all-to-all-done = bf16[16,128,512]{1,2,0:T(8,128)(2,1)S(1)} async-done(((bf16[16,128,512]{1,2,0:T(8,128)(2,1)}), bf16[16,128,512]{1,2,0:T(8,128)(2,1)S(1)}, u32[]{:S(2)}, u32[]{:S(2)}) %all-to-all-start) | async-done | bytes 2097184 | tf_op jit(solution)/shard_map/all_to_all | solution.py:123
  71.4 8.1 %bitcast_reduce_fusion = (f32[128,4,16]{0,2,1:T(8,128)S(1)}, f32[4,512,128,16]{2,1,3,0:T(8,128)}) fusion(pred[512]{0:T(512)(128)(4,1)S(1)} %broadcast_in_dim.133, bf16[128,4,16,128]{0,3,2,1:T(8,128)(2,1)S(1)} %bitcast.114, bf16[512,1,4,128]{3,2,1,0:T(4,128)(2,1)} %get-tuple-element.59), kind=kOutput, calls=%fused_computation.4 | convolution fusion | flops 1086316544 | bytes 19431936 | tf_op jit(solution)/shard_map/while/body/eval_jaxpr/qkgd,rkd->qkgr/dot_general | solution.py:89
  79.5 2.9 %fusion.15 = (f32[128,4,16]{0,2,1:T(8,128)S(1)}, f32[4,136,128,16]{2,1,3,0:T(8,128)}) fusion(pred[128,136]{0,1:T(8,128)(4,1)S(1)} %pad_add_fusion, bf16[128,4,16,128]{0,3,2,1:T(8,128)(2,1)S(1)} %bitcast.115, bf16[128,2,4,128]{3,0,2,1:T(8,128)(2,1)S(1)} %copy_select_fusion, bf16[8,2,4,128]{3,0,2,1:T(8,128)(2,1)S(1)} %copy.131), kind=kOutput, calls=%fused_computation.25 | convolution fusion | flops 288825344 | bytes 6882304 | tf_op jit(solution)/shard_map/while/body/eval_jaxpr/qkgd,rkd->qkgr/dot_general | solution.py:89
  82.4 0.8 broadcast_in_dim.138
  83.2 3.9 %all-to-all-start.2 = ((f32[16,128,4,16]{1,3,2,0:T(8,128)}), f32[16,128,4,16]{1,3,2,0:T(8,128)S(1)}, u32[]{:S(2)}, u32[]{:S(2)}) async-start(f32[16,128,4,16]{1,3,2,0:T(8,128)} %broadcast_in_dim.138), calls=%async_computation.2 | async-start | bytes 1048576 | tf_op jit(solution)/shard_map/all_to_all | solution.py:26
  87.1 8.5 %fusion.2 = f32[128,4,16]{0,2,1:T(8,128)S(1)} fusion(f32[4,512,128,16]{2,1,3,0:T(8,128)} %get-tuple-element.69, f32[128,4,16]{0,2,1:T(8,128)S(1)} %get-tuple-element.62, pred[512]{0:T(512)(128)(4,1)S(1)} %broadcast_in_dim.133), kind=kLoop, calls=%fused_computation.8 | loop fusion | flops 20963328 | bytes 16843264 | tf_op jit(solution)/shard_map/while/body/eval_jaxpr/reduce_sum | solution.py:99
  95.7 1.3 fusion.16
  97.0 5.3 %fusion.17 = f32[4,128,128,16]{2,1,3,0:T(8,128)} fusion(f32[4,136,128,16]{2,1,3,0:T(8,128)S(1)} %bitcast.113, f32[128,4,16]{0,2,1:T(8,128)S(1)} %get-tuple-element.65, pred[128,136]{0,1:T(8,128)(4,1)S(1)} %pad_add_fusion, bf16[8,2,4,128]{3,0,2,1:T(8,128)(2,1)S(1)} %copy.131, bf16[128,2,4,128]{3,0,2,1:T(8,128)(2,1)S(1)} %copy_select_fusion), kind=kOutput, calls=%fused_computation.27 | convolution fusion | flops 1716011008 | bytes 8979456 | tf_op jit(solution)/shard_map/while/body/eval_jaxpr/qkgr,rkd->qkgd/dot_general | solution.py:101
  102.3 15.8 %fusion.13 = f32[128,4,16,128]{0,3,2,1:T(8,128)S(1)} fusion(f32[4,128,128,16]{2,1,3,0:T(8,128)} %fusion.17, f32[4,512,128,16]{2,1,3,0:T(8,128)} %get-tuple-element.69, f32[128,4,16]{0,2,1:T(8,128)S(1)} %get-tuple-element.62, pred[512]{0:T(512)(128)(4,1)S(1)} %broadcast_in_dim.133, f32[128,4,16]{0,2,1:T(8,128)S(1)} %get-tuple-element.64, ...), kind=kOutput, calls=%fused_computation.22 | convolution fusion | flops 6465519616 | bytes 25887232 | tf_op jit(solution)/shard_map/while/body/eval_jaxpr/qkgr,rkd->qkgd/dot_general | solution.py:101
  118.1 2.8 %copy.141 = f32[128,16,4,128]{0,2,3,1:T(4,128)S(1)} copy(f32[128,16,4,128]{0,3,2,1:T(8,128)S(1)} %bitcast.116) | data formatting | bytes 8388608 | tf_op jit(solution)/shard_map/concatenate | solution.py:49
  121.0 3.0 %maximum_bitcast_fusion = f32[16,128,4,129]{1,2,3,0:T(4,128)} fusion(f32[128,16,4,1]{0,2,3,1:T(4,128)S(1)} %exponential_multiply_fusion, f32[128,16,4,128]{0,2,3,1:T(4,128)S(1)} %copy.141), kind=kLoop, calls=%fused_computation.18 | loop fusion | flops 1056768 | bytes 8454144 | tf_op jit(solution)/shard_map/transpose | solution.py:38
  123.9 7.0 %all-to-all-start.3 = ((f32[16,128,4,129]{1,2,3,0:T(4,128)}), f32[16,128,4,129]{1,2,3,0:T(4,128)}, u32[]{:S(2)}, u32[]{:S(2)}) async-start(f32[16,128,4,129]{1,2,3,0:T(4,128)} %maximum_bitcast_fusion), calls=%async_computation.3 | async-start | bytes 8454144 | tf_op jit(solution)/shard_map/all_to_all | solution.py:43
  131.6 0.6 bitcast_dynamic-update-slice_fusion
  132.2 59.9 %all-to-all-done.3 = f32[16,128,4,129]{1,2,3,0:T(4,128)} async-done(((f32[16,128,4,129]{1,2,3,0:T(4,128)}), f32[16,128,4,129]{1,2,3,0:T(4,128)}, u32[]{:S(2)}, u32[]{:S(2)}) %all-to-all-start.3) | async-done | bytes 4227104 | tf_op jit(solution)/shard_map/all_to_all | solution.py:43
  192.1 2.9 %reduce_sum.63 = f32[128,4,129]{0,1,2:T(4,128)S(1)} reduce(f32[16,128,4,129]{1,2,3,0:T(4,128)} %all-to-all-done.3, f32[]{:T(128)} %constant.52.clone.1), dimensions={0}, to_apply=%region_7.8 | reduce | flops 990720 | bytes 4491268 | tf_op jit(solution)/shard_map/reduce_sum | solution.py:44
  195.1 0.8 copy.143
  (32 shorter events, 0.3 us)
Async XLA Ops:
  1.8 4.6 %copy-start = (bf16[1,12,32,2,512]{4,3,2,1,0:T(2,128)(2,1)}, bf16[1,12,32,2,512]{4,3,2,1,0:T(2,128)(2,1)S(1)}, u32[]{:S(2)}) copy-start(bf16[1,12,32,2,512]{4,3,2,1,0:T(2,128)(2,1)S(1)} %copy.173) | copy-start | bytes 2359300
  6.3 9.1 %copy-start.1 = (bf16[1,128,512]{2,1,0:T(8,128)(2,1)S(1)}, bf16[1,128,512]{2,1,0:T(8,128)(2,1)}, u32[]{:S(2)}) copy-start(bf16[1,128,512]{2,1,0:T(8,128)(2,1)} %param.8) | copy-start | bytes 393220
  9.9 31.0 %copy-start.3 = (s32[1,4]{1,0:T(1,128)S(1)}, s32[1,4]{1,0:T(1,128)}, u32[]{:S(2)}) copy-start(s32[1,4]{1,0:T(1,128)} %param.11) | copy-start | bytes 52
  9.9 31.2 %copy-start.2 = (bf16[1,8,2,512]{3,2,1,0:T(2,128)(2,1)S(1)}, bf16[1,8,2,512]{3,2,1,0:T(2,128)(2,1)}, u32[]{:S(2)}) copy-start(bf16[1,8,2,512]{3,2,1,0:T(2,128)(2,1)} %param.9) | copy-start | bytes 49156
  9.9 21.5 %all-to-all-start.1 = ((bf16[8,2,32769]{2,1,0:T(2,128)(2,1)}), bf16[8,2,32769]{2,1,0:T(2,128)(2,1)S(1)}, u32[]{:S(2)}, u32[]{:S(2)}) async-start(bf16[8,2,32769]{2,1,0:T(2,128)(2,1)} %pad_maximum_fusion), calls=%async_computation.1 | async-start | bytes 2105344 | tf_op jit(solution)/shard_map/all_to_all | solution.py:17
  33.2 38.2 %all-to-all-start = ((bf16[16,128,512]{1,2,0:T(8,128)(2,1)}), bf16[16,128,512]{1,2,0:T(8,128)(2,1)S(1)}, u32[]{:S(2)}, u32[]{:S(2)}) async-start(bf16[16,128,512]{1,2,0:T(8,128)(2,1)} %stack.3), calls=%async_computation | async-start | bytes 4194304 | tf_op jit(solution)/shard_map/all_to_all | solution.py:123
  83.2 12.5 %slice-start = ((s8[4456448]{0:T(1024)(128)(4,1)}), s8[262144]{0:T(1024)(128)(4,1)S(1)}, s32[]{:S(2)}) async-start(s8[4456448]{0:T(1024)(128)(4,1)} %bitcast.112), calls=%async_computation.4 | async-start | bytes 524288
  83.2 19.0 %all-to-all-start.2 = ((f32[16,128,4,16]{1,3,2,0:T(8,128)}), f32[16,128,4,16]{1,3,2,0:T(8,128)S(1)}, u32[]{:S(2)}, u32[]{:S(2)}) async-start(f32[16,128,4,16]{1,3,2,0:T(8,128)} %broadcast_in_dim.138), calls=%async_computation.2 | async-start | bytes 1048576 | tf_op jit(solution)/shard_map/all_to_all | solution.py:26
  87.1 8.6 %slice-start.1 = ((s8[4456448]{0:T(1024)(128)(4,1)}), s8[4194304]{0:T(1024)(128)(4,1)S(1)}, s32[]{:S(2)}) async-start(s8[4456448]{0:T(1024)(128)(4,1)} %bitcast.112), calls=%async_computation.5 | async-start | bytes 8388608
  123.9 68.2 %all-to-all-start.3 = ((f32[16,128,4,129]{1,2,3,0:T(4,128)}), f32[16,128,4,129]{1,2,3,0:T(4,128)}, u32[]{:S(2)}, u32[]{:S(2)}) async-start(f32[16,128,4,129]{1,2,3,0:T(4,128)} %maximum_bitcast_fusion), calls=%async_computation.3 | async-start | bytes 8454144 | tf_op jit(solution)/shard_map/all_to_all | solution.py:43
